TPU v7x, 1024 devices: a whole 8x8x8 slice. The times are simulated.
1024 devices in a mesh: bag: 64 (over y_lo, z, core), ulysses: 16 (over x, y_hi).
Axes of the slice: x: 8, y: 8 (y_hi: 2, y_lo: 4; y = y_hi * 4 + y_lo), z: 8, core: 2. Of those that a mesh axis runs over, the one named last changes fastest.
Arguments:
- queries: bfloat16 [65536, 4096], P(('bag', 'ulysses')), may hold values from -13 to 13
- keys: bfloat16 [65536, 4096], P(('bag', 'ulysses')), may hold values from -13 to 13
- values: bfloat16 [65536, 4096], P(('bag', 'ulysses')), may hold values from -6 to 6
- span_route: int32 [64, 16, 64], P('bag'), may hold values from 0 to 63, each once within a row
- seq_lengths: int32 [64, 4], P('bag'), may hold values from 1 to 512, 1024 in all within a row
Outputs:
- attended: bfloat16 [65536, 4096], P(('bag', 'ulysses'))
Inputs may be any that keep to these rules, and one draw needn't show every extreme that they name: For each b and u, span_route[b, u, 0 to 63] is a permutation of the bags. `seq_lengths`: row B lists bag B's 4 sequence lengths in packed order; each row sums to 1024 and its largest entry is 512.
All inputs are finite; a program needn't handle non-finite values.
Results may differ from a plain program's by a relative error of at most 0.0049.
Values may be sent and summed in bfloat16 or wider, within the bound.
A program may use at most 32 MiB of HBM per device.

v0:
```python
import math

import jax
import jax.numpy as jnp
from jax import lax
from jax.sharding import PartitionSpec as P

HEADS = 32
HDIM = 128


def build_sequence(lengths, bag_tok):
    seq_ends = jnp.cumsum(lengths)
    positions = jnp.arange(bag_tok, dtype=jnp.int32)
    return jnp.sum((positions[:, None] >= seq_ends[None, :]).astype(jnp.int32), axis=1)


def attend_local(query_rows, key_rows, value_rows, sequence, heads_here):
    bag_tok = query_rows.shape[0]
    head_cols = heads_here * HDIM
    block_rows = min(512, bag_tok)
    block_count = bag_tok // block_rows
    score_scale = 1.0 / math.sqrt(HDIM)
    query_heads = query_rows.reshape(bag_tok, heads_here, HDIM)
    key_heads = key_rows.reshape(bag_tok, heads_here, HDIM)
    value_heads = value_rows.reshape(bag_tok, heads_here, HDIM)

    def one_block(block_index, result):
        first_row = block_index * block_rows
        query_block = lax.dynamic_slice_in_dim(query_heads, first_row, block_rows, 0)
        query_seq = lax.dynamic_slice_in_dim(sequence, first_row, block_rows, 0)
        scores = (
            jnp.einsum("qhd,khd->hqk", query_block, key_heads, preferred_element_type=jnp.float32)
            * score_scale
        )
        scores = jnp.where((query_seq[:, None] == sequence[None, :])[None, :, :], scores, -jnp.inf)
        row_max = jnp.max(scores, axis=-1, keepdims=True)
        expo = jnp.exp(scores - row_max)
        weights = (expo / jnp.sum(expo, axis=-1, keepdims=True)).astype(jnp.bfloat16)
        output = jnp.einsum(
            "hqk,khd->qhd", weights, value_heads, preferred_element_type=jnp.float32
        )
        output = output.astype(jnp.bfloat16).reshape(block_rows, head_cols)
        return lax.dynamic_update_slice_in_dim(result, output, first_row, 0)

    return lax.fori_loop(0, block_count, one_block, jnp.zeros((bag_tok, head_cols), jnp.bfloat16))


def shards(queries, keys, values, span_route, seq_lengths):
    bag_count = lax.axis_size("bag")
    group_count = lax.axis_size("ulysses")
    tok_dev, row_width = queries.shape
    span_len = tok_dev // bag_count
    heads_here = HEADS // group_count
    head_cols = heads_here * HDIM
    bag_tok = tok_dev * group_count
    route_rows = span_route[0]
    column = jnp.arange(bag_count, dtype=jnp.int32)
    inverse_all = jnp.sum(
        jnp.where(route_rows[:, None, :] == column[None, :, None], column[None, None, :], 0), axis=2
    )
    my_group = lax.axis_index("ulysses")
    route_mine = lax.dynamic_index_in_dim(route_rows, my_group, 0, keepdims=False)
    inverse_mine = lax.dynamic_index_in_dim(inverse_all, my_group, 0, keepdims=False)

    def to_slots(rows):
        return jnp.take(rows.reshape(bag_count, span_len, row_width), inverse_mine, axis=0)

    arrived = (
        lax.all_to_all(to_slots(queries), "bag", split_axis=0, concat_axis=0, tiled=True),
        lax.all_to_all(to_slots(keys), "bag", split_axis=0, concat_axis=0, tiled=True),
        lax.all_to_all(to_slots(values), "bag", split_axis=0, concat_axis=0, tiled=True),
    )

    def split_cols(rows):
        return rows.reshape(bag_count * span_len, group_count, head_cols)

    packed = (
        lax.all_to_all(split_cols(arrived[0]), "ulysses", split_axis=1, concat_axis=0, tiled=True),
        lax.all_to_all(split_cols(arrived[1]), "ulysses", split_axis=1, concat_axis=0, tiled=True),
        lax.all_to_all(split_cols(arrived[2]), "ulysses", split_axis=1, concat_axis=0, tiled=True),
    )
    sequence = build_sequence(seq_lengths[0], bag_tok)
    attended_bag = attend_local(
        packed[0].reshape(bag_tok, head_cols),
        packed[1].reshape(bag_tok, head_cols),
        packed[2].reshape(bag_tok, head_cols),
        sequence,
        heads_here,
    )
    merged = lax.all_to_all(
        attended_bag.reshape(group_count, bag_count * span_len, head_cols),
        "ulysses",
        split_axis=0,
        concat_axis=2,
        tiled=True,
    )
    returned = lax.all_to_all(
        merged.reshape(bag_count, span_len, row_width),
        "bag",
        split_axis=0,
        concat_axis=0,
        tiled=True,
    )
    result = jnp.take(returned, route_mine, axis=0)
    return result.reshape(tok_dev, row_width)


def solution(mesh):
    placed = (
        P(("bag", "ulysses"), None),
        P(("bag", "ulysses"), None),
        P(("bag", "ulysses"), None),
        P("bag", None, None),
        P("bag", None),
    )
    return jax.shard_map(
        shards, mesh=mesh, in_specs=placed, out_specs=P(("bag", "ulysses"), None), check_vma=False
    )
```

profile of v0, /device:TPU:1, one launch (start us, length us, event | category | flops | bytes accessed | tf_op | source)
XLA Modules:
  0.0 250.3 jit_solution(8858329635562881383)
XLA Ops:
  7.4 22.1 %all-to-all-start.2 = ((bf16[64,2,2048]{2,1,0:T(2,128)(2,1)}), bf16[64,2,2048]{2,1,0:T(2,128)(2,1)S(1)}, u32[]{:S(2)}, u32[]{:S(2)}) async-start(bf16[64,2,2048]{2,1,0:T(2,128)(2,1)} %reshape.201), calls=%async_computation.2 | async-start | bytes 1048576 | tf_op jit(solution)/shard_map/all_to_all | solution.py:71
  32.6 13.9 %all-to-all-done.2 = bf16[64,2,2048]{2,1,0:T(2,128)(2,1)S(1)} async-done(((bf16[64,2,2048]{2,1,0:T(2,128)(2,1)}), bf16[64,2,2048]{2,1,0:T(2,128)(2,1)S(1)}, u32[]{:S(2)}, u32[]{:S(2)}) %all-to-all-start.2) | async-done | bytes 524320 | tf_op jit(solution)/shard_map/all_to_all | solution.py:71
  46.6 6.2 %all-to-all-start.4 = ((bf16[64,2,2048]{2,1,0:T(2,128)(2,1)}), bf16[64,2,2048]{2,1,0:T(2,128)(2,1)S(1)}, u32[]{:S(2)}, u32[]{:S(2)}) async-start(bf16[64,2,2048]{2,1,0:T(2,128)(2,1)} %reshape.203), calls=%async_computation.4 | async-start | bytes 1048576 | tf_op jit(solution)/shard_map/all_to_all | solution.py:72
  54.8 15.0 %all-to-all-done.4 = bf16[64,2,2048]{2,1,0:T(2,128)(2,1)S(1)} async-done(((bf16[64,2,2048]{2,1,0:T(2,128)(2,1)}), bf16[64,2,2048]{2,1,0:T(2,128)(2,1)S(1)}, u32[]{:S(2)}, u32[]{:S(2)}) %all-to-all-start.4) | async-done | bytes 524320 | tf_op jit(solution)/shard_map/all_to_all | solution.py:72
  69.8 6.2 %all-to-all-start = ((bf16[64,2,2048]{2,1,0:T(2,128)(2,1)}), bf16[64,2,2048]{2,1,0:T(2,128)(2,1)S(1)}, u32[]{:S(2)}, u32[]{:S(2)}) async-start(bf16[64,2,2048]{2,1,0:T(2,128)(2,1)} %reshape.199), calls=%async_computation | async-start | bytes 1048576 | tf_op jit(solution)/shard_map/all_to_all | solution.py:70
  76.5 3.1 %reduce.1 = bf16[64,4096]{1,0:T(8,128)(2,1)S(1)} reduce(bf16[64,1,4096]{2,1,0:T(2,128)(2,1)S(1)} %reshape.202, bf16[]{:T(256)} %constant.80), dimensions={1}, to_apply=%all_to_all.60.reduce_sub_computation | reduce | bytes 1048578 | tf_op jit(solution)/shard_map/all_to_all | solution.py:71
  80.5 12.5 %all-to-all-done = bf16[64,2,2048]{2,1,0:T(2,128)(2,1)S(1)} async-done(((bf16[64,2,2048]{2,1,0:T(2,128)(2,1)}), bf16[64,2,2048]{2,1,0:T(2,128)(2,1)S(1)}, u32[]{:S(2)}, u32[]{:S(2)}) %all-to-all-start) | async-done | bytes 524320 | tf_op jit(solution)/shard_map/all_to_all | solution.py:70
  93.0 9.6 %all-to-all-start.3 = ((bf16[64,16,256]{2,0,1:T(8,128)(2,1)}), bf16[64,16,256]{2,0,1:T(8,128)(2,1)S(1)}, u32[]{:S(2)}, u32[]{:S(2)}) async-start(bf16[64,16,256]{2,0,1:T(8,128)(2,1)} %bitcast.69), calls=%async_computation.3 | async-start | bytes 1048576 | tf_op jit(solution)/shard_map/all_to_all | solution.py:80
  103.2 3.1 %reduce.2 = bf16[64,4096]{1,0:T(8,128)(2,1)S(1)} reduce(bf16[64,1,4096]{2,1,0:T(2,128)(2,1)S(1)} %reshape.204, bf16[]{:T(256)} %constant.80), dimensions={1}, to_apply=%all_to_all.64.reduce_sub_computation | reduce | bytes 1048578 | tf_op jit(solution)/shard_map/all_to_all | solution.py:72
  107.2 16.4 %all-to-all-done.3 = bf16[64,16,256]{2,0,1:T(8,128)(2,1)S(1)} async-done(((bf16[64,16,256]{2,0,1:T(8,128)(2,1)}), bf16[64,16,256]{2,0,1:T(8,128)(2,1)S(1)}, u32[]{:S(2)}, u32[]{:S(2)}) %all-to-all-start.3) | async-done | bytes 524320 | tf_op jit(solution)/shard_map/all_to_all | solution.py:80
  123.6 6.2 %all-to-all-start.5 = ((bf16[64,16,256]{2,0,1:T(8,128)(2,1)}), bf16[64,16,256]{2,0,1:T(8,128)(2,1)S(1)}, u32[]{:S(2)}, u32[]{:S(2)}) async-start(bf16[64,16,256]{2,0,1:T(8,128)(2,1)} %bitcast.68), calls=%async_computation.5 | async-start | bytes 1048576 | tf_op jit(solution)/shard_map/all_to_all | solution.py:81
  130.4 3.1 %reduce = bf16[64,4096]{1,0:T(8,128)(2,1)S(1)} reduce(bf16[64,1,4096]{2,1,0:T(2,128)(2,1)S(1)} %reshape.200, bf16[]{:T(256)} %constant.80), dimensions={1}, to_apply=%all_to_all.56.reduce_sub_computation | reduce | bytes 1048578 | tf_op jit(solution)/shard_map/all_to_all | solution.py:70
  134.4 16.0 %all-to-all-done.5 = bf16[64,16,256]{2,0,1:T(8,128)(2,1)S(1)} async-done(((bf16[64,16,256]{2,0,1:T(8,128)(2,1)}), bf16[64,16,256]{2,0,1:T(8,128)(2,1)S(1)}, u32[]{:S(2)}, u32[]{:S(2)}) %all-to-all-start.5) | async-done | bytes 524320 | tf_op jit(solution)/shard_map/all_to_all | solution.py:81
  150.4 6.3 %all-to-all-start.1 = ((bf16[64,16,256]{2,0,1:T(8,128)(2,1)}), bf16[64,16,256]{2,0,1:T(8,128)(2,1)S(1)}, u32[]{:S(2)}, u32[]{:S(2)}) async-start(bf16[64,16,256]{2,0,1:T(8,128)(2,1)} %bitcast.70), calls=%async_computation.1 | async-start | bytes 1048576 | tf_op jit(solution)/shard_map/all_to_all | solution.py:79
  158.4 18.6 %all-to-all-done.1 = bf16[64,16,256]{2,0,1:T(8,128)(2,1)S(1)} async-done(((bf16[64,16,256]{2,0,1:T(8,128)(2,1)}), bf16[64,16,256]{2,0,1:T(8,128)(2,1)S(1)}, u32[]{:S(2)}, u32[]{:S(2)}) %all-to-all-start.1) | async-done | bytes 524320 | tf_op jit(solution)/shard_map/all_to_all | solution.py:79
  177.2 15.2 %while.13 = (s32[]{:T(128)}, bf16[1024,256]{1,0:T(8,128)(2,1)S(1)}, s32[1024]{0:T(1024)S(1)}, bf16[1024,2,128]{2,1,0:T(2,128)(2,1)S(1)}, bf16[1024,2,128]{2,0,1:...) while((s32[]{:T(128)}, bf16[1024,256]{1,0:T(8,128)(2,1)S(1)}, ...), condition=%wide.region_6.8_spmd, body=%wide.region_3.7_spmd.sunk | while | flops 543818752 | bytes 12601503 | solution.py:46
  177.9 3.5 %fusion.35 = (f32[2,512]{1,0:T(2,128)S(1)}, f32[2,512,1024]{2,1,0:T(8,128)}) fusion(pred[512,1024]{1,0:T(8,128)(4,1)S(1)} %broadcast_compare_fusion.2, bf16[1024,2,128]{2,0,1:T(8,128)(2,1)S(1)} %get-tuple-element.232, bf16[512,2,128]{2,1,0:T(2,128)(2,1)S(1)} %constant_dynamic-slice_fusion.2), kind=kOutput, calls=%fused_computation.42.clone.1 | convolution fusion | flops 272630784 | bytes 5509120 | tf_op jit(solution)/shard_map/while/body/eval_jaxpr/sub | solution.py:38
  181.4 3.2 %fusion.36 = bf16[2,512,128]{1,2,0:T(8,128)(2,1)S(1)} fusion(bf16[1024,2,128]{0,2,1:T(8,128)(2,1)} %get-tuple-element.233, f32[2,512,1024]{2,1,0:T(8,128)} %get-tuple-element.206, f32[2,512]{1,0:T(2,128)S(1)} %get-tuple-element.207), kind=kOutput, calls=%fused_computation.13.clone.1 | convolution fusion | flops 270663680 | bytes 4984832 | tf_op jit(solution)/shard_map/while/body/eval_jaxpr/hqk,khd->qhd/dot_general | solution.py:40
  185.4 3.5 %fusion.35 = (f32[2,512]{1,0:T(2,128)S(1)}, f32[2,512,1024]{2,1,0:T(8,128)}) fusion(pred[512,1024]{1,0:T(8,128)(4,1)S(1)} %broadcast_compare_fusion.2, bf16[1024,2,128]{2,0,1:T(8,128)(2,1)S(1)} %get-tuple-element.232, bf16[512,2,128]{2,1,0:T(2,128)(2,1)S(1)} %constant_dynamic-slice_fusion.2), kind=kOutput, calls=%fused_computation.42.clone.1 | convolution fusion | flops 272630784 | bytes 5509120 | tf_op jit(solution)/shard_map/while/body/eval_jaxpr/sub | solution.py:38
  189.0 3.2 %fusion.36 = bf16[2,512,128]{1,2,0:T(8,128)(2,1)S(1)} fusion(bf16[1024,2,128]{0,2,1:T(8,128)(2,1)} %get-tuple-element.233, f32[2,512,1024]{2,1,0:T(8,128)} %get-tuple-element.206, f32[2,512]{1,0:T(2,128)S(1)} %get-tuple-element.207), kind=kOutput, calls=%fused_computation.13.clone.1 | convolution fusion | flops 270663680 | bytes 4984832 | tf_op jit(solution)/shard_map/while/body/eval_jaxpr/hqk,khd->qhd/dot_general | solution.py:40
  192.4 25.4 %all_to_all.80 = bf16[16,64,256]{2,1,0:T(8,128)(2,1)S(1)} all-to-all(bf16[16,64,256]{2,1,0:T(8,128)(2,1)S(1)} %bitcast.83), channel_id=1, replica_groups=mesh['bag'=64,'ulysses'=16] {'ulysses'}, dimensions={0} | all-to-all | bytes 1048576 | tf_op jit(solution)/shard_map/all_to_all | solution.py:91
  218.3 3.7 %reduce.6 = bf16[64,4096]{1,0:T(8,128)(2,1)S(1)} reduce(bf16[64,1,4096]{2,1,0:T(2,128)(2,1)S(1)} %reshape.195, bf16[]{:T(256)} %broadcast.80), dimensions={1}, to_apply=%reshape.195.reduce_sub_computation | reduce | bytes 1048578 | tf_op jit(solution)/shard_map/reshape | solution.py:99
  223.1 7.2 %all-to-all-start.7 = ((bf16[64,2,2048]{2,1,0:T(2,128)(2,1)}), bf16[64,2,2048]{2,1,0:T(2,128)(2,1)S(1)}, u32[]{:S(2)}, u32[]{:S(2)}) async-start(bf16[64,2,2048]{2,1,0:T(2,128)(2,1)} %reshape.205), calls=%async_computation.7 | async-start | bytes 1048576 | tf_op jit(solution)/shard_map/all_to_all | solution.py:98
  231.1 16.3 %all-to-all-done.7 = bf16[64,2,2048]{2,1,0:T(2,128)(2,1)S(1)} async-done(((bf16[64,2,2048]{2,1,0:T(2,128)(2,1)}), bf16[64,2,2048]{2,1,0:T(2,128)(2,1)S(1)}, u32[]{:S(2)}, u32[]{:S(2)}) %all-to-all-start.7) | async-done | bytes 524320 | tf_op jit(solution)/shard_map/all_to_all | solution.py:98
  (55 shorter events, 25.4 us)
Async XLA Ops:
  0.0 1.2 copy-start
  0.0 2.1 copy-start.1
  1.2 1.8 copy-start.2
  7.4 39.2 %all-to-all-start.2 = ((bf16[64,2,2048]{2,1,0:T(2,128)(2,1)}), bf16[64,2,2048]{2,1,0:T(2,128)(2,1)S(1)}, u32[]{:S(2)}, u32[]{:S(2)}) async-start(bf16[64,2,2048]{2,1,0:T(2,128)(2,1)} %reshape.201), calls=%async_computation.2 | async-start | bytes 1048576 | tf_op jit(solution)/shard_map/all_to_all | solution.py:71
  46.6 23.2 %all-to-all-start.4 = ((bf16[64,2,2048]{2,1,0:T(2,128)(2,1)}), bf16[64,2,2048]{2,1,0:T(2,128)(2,1)S(1)}, u32[]{:S(2)}, u32[]{:S(2)}) async-start(bf16[64,2,2048]{2,1,0:T(2,128)(2,1)} %reshape.203), calls=%async_computation.4 | async-start | bytes 1048576 | tf_op jit(solution)/shard_map/all_to_all | solution.py:72
  69.8 23.2 %all-to-all-start = ((bf16[64,2,2048]{2,1,0:T(2,128)(2,1)}), bf16[64,2,2048]{2,1,0:T(2,128)(2,1)S(1)}, u32[]{:S(2)}, u32[]{:S(2)}) async-start(bf16[64,2,2048]{2,1,0:T(2,128)(2,1)} %reshape.199), calls=%async_computation | async-start | bytes 1048576 | tf_op jit(solution)/shard_map/all_to_all | solution.py:70
  93.0 30.6 %all-to-all-start.3 = ((bf16[64,16,256]{2,0,1:T(8,128)(2,1)}), bf16[64,16,256]{2,0,1:T(8,128)(2,1)S(1)}, u32[]{:S(2)}, u32[]{:S(2)}) async-start(bf16[64,16,256]{2,0,1:T(8,128)(2,1)} %bitcast.69), calls=%async_computation.3 | async-start | bytes 1048576 | tf_op jit(solution)/shard_map/all_to_all | solution.py:80
  103.2 53.5 %copy-start.3 = (s32[1,4]{1,0:T(1,128)S(1)}, s32[1,4]{1,0:T(1,128)}, u32[]{:S(2)}) copy-start(s32[1,4]{1,0:T(1,128)} %param.13) | copy-start | bytes 52
  123.6 26.8 %all-to-all-start.5 = ((bf16[64,16,256]{2,0,1:T(8,128)(2,1)}), bf16[64,16,256]{2,0,1:T(8,128)(2,1)S(1)}, u32[]{:S(2)}, u32[]{:S(2)}) async-start(bf16[64,16,256]{2,0,1:T(8,128)(2,1)} %bitcast.68), calls=%async_computation.5 | async-start | bytes 1048576 | tf_op jit(solution)/shard_map/all_to_all | solution.py:81
  150.4 26.6 %all-to-all-start.1 = ((bf16[64,16,256]{2,0,1:T(8,128)(2,1)}), bf16[64,16,256]{2,0,1:T(8,128)(2,1)S(1)}, u32[]{:S(2)}, u32[]{:S(2)}) async-start(bf16[64,16,256]{2,0,1:T(8,128)(2,1)} %bitcast.70), calls=%async_computation.1 | async-start | bytes 1048576 | tf_op jit(solution)/shard_map/all_to_all | solution.py:79
  223.1 24.3 %all-to-all-start.7 = ((bf16[64,2,2048]{2,1,0:T(2,128)(2,1)}), bf16[64,2,2048]{2,1,0:T(2,128)(2,1)S(1)}, u32[]{:S(2)}, u32[]{:S(2)}) async-start(bf16[64,2,2048]{2,1,0:T(2,128)(2,1)} %reshape.205), calls=%async_computation.7 | async-start | bytes 1048576 | tf_op jit(solution)/shard_map/all_to_all | solution.py:98
where the time goes:
time: 251 us; the launch traced here: 250 us
  waiting for transfers between devices  109 us (43%)
  starting transfers between devices  63.7 us (25%)
  blocking collectives  25.4 us (10%)
  other arithmetic  21.6 us (9%)
  local copies, waits for them, and re-layouts  16.9 us (7%)
  matrix products  13.5 us (5%)
    all_to_all x1, blocking collectives, shards(): lax.all_to_all(attended_bag.reshape(group_count, bag_count * span_len, he...  25.4 us
    all_to_all x1, starting transfers between devices, shards(): lax.all_to_all(to_slots(keys), 'bag', split_axis=0, concat_axis=0, tiled=...  22.1 us
    all_to_all x1, waiting for transfers between devices, shards(): lax.all_to_all(split_cols(arrived[0]), 'ulysses', split_axis=1, concat_ax...  18.6 us
    all_to_all x1, waiting for transfers between devices, shards(): lax.all_to_all(split_cols(arrived[1]), 'ulysses', split_axis=1, concat_ax...  16.4 us
    all_to_all x1, waiting for transfers between devices, shards(): lax.all_to_all(merged.reshape(bag_count, span_len, row_width), 'bag', spl...  16.3 us
    all_to_all x1, waiting for transfers between devices, shards(): lax.all_to_all(split_cols(arrived[2]), 'ulysses', split_axis=1, concat_ax...  16 us
    all_to_all x1, waiting for transfers between devices, shards(): lax.all_to_all(to_slots(values), 'bag', split_axis=0, concat_axis=0, tile...  15 us
    all_to_all x1, waiting for transfers between devices, shards(): lax.all_to_all(to_slots(keys), 'bag', split_axis=0, concat_axis=0, tiled=...  13.9 us
  transfers between devices with their start and end apart: 7, of which 7 were waited for; matrix products, arithmetic and copies ran while one was open for 8% of the time, Pallas kernels for 0%

commit v1 on v0

v1 whole, which is shorter than its diff:
```python
import functools
import math

import jax
import jax.numpy as jnp
from jax import lax
from jax.experimental import pallas as pl
from jax.experimental.pallas import tpu as pltpu
from jax.sharding import PartitionSpec as P

HEADS = 32
HDIM = 128
NX, NY, NZ = 8, 8, 16
UNIT = (2, HDIM)
BLOCK = (NX, NY, NZ) + UNIT
MESH = pl.DeviceIdType.MESH
VMEM = pl.BlockSpec(memory_space=pltpu.VMEM)
SMEM = pl.BlockSpec(memory_space=pltpu.SMEM)


def pack_kernel(route_ref, *refs):
    ins, outs = refs[:3], refs[3:]
    lane_route = jnp.concatenate([route_ref[...], route_ref[...]], axis=1)
    row = lax.broadcasted_iota(jnp.int32, (128, 128), 0)
    lane = lax.broadcasted_iota(jnp.int32, (128, 128), 1)
    pick = ((lane_route == row // 2) & (lane // 64 == row % 2)).astype(jnp.bfloat16)
    for i_ref, o_ref in zip(ins, outs):
        for u in range(16):
            pair = jnp.concatenate(
                [i_ref[:, u * 256 : u * 256 + 128], i_ref[:, u * 256 + 128 : u * 256 + 256]], axis=0
            )
            rows = jnp.dot(pick, pair, preferred_element_type=jnp.float32)
            o_ref[u * 128 : (u + 1) * 128, :] = rows.astype(jnp.bfloat16)


def unpack_kernel(route_ref, i_ref, o_ref):
    col = route_ref[...]
    lane = lax.broadcasted_iota(jnp.int32, (64, 128), 1)
    picks = [(lane == col * 2 + h).astype(jnp.bfloat16) for h in (0, 1)]
    pick = jnp.concatenate(picks, axis=0)
    for u in range(16):
        both = jnp.dot(
            pick, i_ref[u * 128 : (u + 1) * 128, :], preferred_element_type=jnp.float32
        ).astype(jnp.bfloat16)
        o_ref[:, u * 256 : u * 256 + 128] = both[:64]
        o_ref[:, u * 256 + 128 : u * 256 + 256] = both[64:]


def place():
    b = lax.axis_index("bag")
    u = lax.axis_index("ulysses")
    return {"x": u // 2, "y": (u % 2) * 4 + b // 16, "z": b % 16}


def device(here, axis, t):
    at = dict(here)
    at[axis] = t
    return ((at["y"] % 4) * 16 + at["z"], at["x"] * 2 + at["y"] // 4)


def slot(ref, axis, t):
    if axis == "x":
        return ref.at[t]
    if axis == "y":
        return ref.at[:, t]
    return ref.at[:, :, t]


SIZE = {"x": NX, "y": NY, "z": NZ}
STEPS = {"x": (4, 3, 5, 2, 6, 1, 7), "y": (4, 3, 5, 2, 6, 1, 7)}
STEPS["z"] = (8, 9, 7, 6, 10, 5, 11, 4, 12, 3, 13, 2, 14, 1, 15)


def exchange_start(axis, here, src, dst, send, recv, own):
    mine = here[axis]
    for step in STEPS[axis]:
        t = (mine + step) % SIZE[axis]
        pltpu.make_async_remote_copy(
            src_ref=slot(src, axis, t),
            dst_ref=slot(dst, axis, mine),
            send_sem=send,
            recv_sem=recv,
            device_id=device(here, axis, t),
            device_id_type=MESH,
        ).start()
    pltpu.make_async_copy(slot(src, axis, mine), slot(dst, axis, mine), own).start()


def exchange_wait(axis, here, src, dst, send, recv, own):
    mine = here[axis]
    part = slot(dst, axis, pl.ds(0, SIZE[axis] - 1))
    pltpu.make_async_copy(part, part, recv).wait()
    pltpu.make_async_copy(part, part, send).wait()
    pltpu.make_async_copy(slot(src, axis, mine), slot(dst, axis, mine), own).wait()


def exchange_kernel(orders, *refs):
    n = len(orders)
    bufs = [refs[:n], refs[2 * n : 3 * n], refs[3 * n : 4 * n], refs[n : 2 * n]]
    send, recv, own = refs[4 * n :]
    here = place()
    barrier = pltpu.get_barrier_semaphore()
    for axis in "xyz":
        for step in STEPS[axis]:
            t = (here[axis] + step) % SIZE[axis]
            pl.semaphore_signal(
                barrier, inc=1, device_id=device(here, axis, t), device_id_type=MESH
            )
    pl.semaphore_wait(barrier, sum(len(steps) for steps in STEPS.values()))
    for stage in range(3):
        for i in range(n):
            exchange_start(
                orders[i][stage], here, bufs[stage][i], bufs[stage + 1][i],
                send.at[i, stage], recv.at[i, stage], own.at[i, stage],
            )
        for i in range(n):
            exchange_wait(
                orders[i][stage], here, bufs[stage][i], bufs[stage + 1][i],
                send.at[i, stage], recv.at[i, stage], own.at[i, stage],
            )


def exchange(orders, collective_id, *arrays):
    n = len(orders)
    shape = jax.ShapeDtypeStruct(BLOCK, jnp.bfloat16)
    return pl.pallas_call(
        functools.partial(exchange_kernel, orders),
        out_shape=[shape] * n,
        in_specs=[VMEM] * n,
        out_specs=[VMEM] * n,
        scratch_shapes=[pltpu.VMEM(BLOCK, jnp.bfloat16)] * (2 * n)
        + [pltpu.SemaphoreType.DMA((n, 3))] * 3,
        compiler_params=pltpu.CompilerParams(has_side_effects=True, collective_id=collective_id),
        name="exchange_" + "_".join(orders),
    )(*[a.reshape(BLOCK) for a in arrays])


def attend_kernel(len_ref, q_ref, k_ref, v_ref, o_ref, qf, kf, vf, of):
    tok = q_ref.shape[0] // 2
    rows = 256
    scale = 1.0 / math.sqrt(HDIM)
    qf[...] = q_ref[...].astype(jnp.float32)
    kf[...] = k_ref[...].astype(jnp.float32)
    vf[...] = v_ref[...].astype(jnp.float32)
    ends = [len_ref[0, 0]]
    for e in range(1, 4):
        ends.append(ends[-1] + len_ref[0, e])

    def sequence(shape, axis, first):
        p = lax.broadcasted_iota(jnp.int32, shape, axis) + first
        return sum((p >= e).astype(jnp.int32) for e in ends)

    key_seq = sequence((1, tok), 1, 0)
    for h in range(2):
        keys = kf[pl.ds(h, tok, stride=2), :].astype(jnp.bfloat16)
        values = vf[pl.ds(h, tok, stride=2), :].astype(jnp.bfloat16)

        def one(i, _, h=h, keys=keys, values=values):
            first = pl.multiple_of(i * rows, rows)
            q = qf[pl.ds(first * 2 + h, rows, stride=2), :].astype(jnp.bfloat16)
            s = lax.dot_general(
                q, keys, (((1,), (1,)), ((), ())), preferred_element_type=jnp.float32
            ) * scale
            same = sequence((rows, 1), 0, first) == key_seq
            s = jnp.where(same, s, -jnp.inf)
            e = jnp.exp(s - jnp.max(s, axis=1, keepdims=True))
            w = (e / jnp.sum(e, axis=1, keepdims=True)).astype(jnp.bfloat16)
            o = jnp.dot(w, values, preferred_element_type=jnp.float32)
            of[pl.ds(first * 2 + h, rows, stride=2), :] = o
            return 0

        lax.fori_loop(0, tok // rows, one, 0)
    o_ref[...] = of[...].astype(jnp.bfloat16)


def shards(queries, keys, values, span_route, seq_lengths):
    route = lax.dynamic_index_in_dim(span_route[0], lax.axis_index("ulysses"), 0, keepdims=True)
    rows = jax.ShapeDtypeStruct((2048, HDIM), jnp.bfloat16)
    units = pl.pallas_call(
        pack_kernel, out_shape=[rows] * 3, in_specs=[VMEM] * 4, out_specs=[VMEM] * 3, name="pack"
    )(route, queries, keys, values)
    q, k, v = exchange(("xyz", "yzx", "zxy"), 1, *units)
    wide = pltpu.VMEM((2048, HDIM), jnp.float32)
    attended = pl.pallas_call(
        attend_kernel,
        out_shape=rows,
        in_specs=[SMEM] + [VMEM] * 3,
        out_specs=VMEM,
        scratch_shapes=[wide] * 4,
        name="attend",
    )(seq_lengths, *[a.reshape(2048, HDIM) for a in (q, k, v)])
    (back,) = exchange(("xyz",), 2, attended)
    return pl.pallas_call(
        unpack_kernel,
        out_shape=jax.ShapeDtypeStruct(queries.shape, jnp.bfloat16),
        in_specs=[VMEM] * 2,
        out_specs=VMEM,
        name="unpack",
    )(route.reshape(64, 1), back.reshape(2048, HDIM))


def solution(mesh):
    placed = (
        P(("bag", "ulysses"), None),
        P(("bag", "ulysses"), None),
        P(("bag", "ulysses"), None),
        P("bag", None, None),
        P("bag", None),
    )
    return jax.shard_map(
        shards, mesh=mesh, in_specs=placed, out_specs=P(("bag", "ulysses"), None), check_vma=False
    )
```

time: 251 us -> 128 us (0.51)
  Pallas kernels: 0 us -> 126 us
  waiting for transfers between devices: 109 us -> 0 us
  starting transfers between devices: 63.7 us -> 0 us
  blocking collectives: 25.4 us -> 0 us
  other arithmetic: 21.6 us -> 0 us
  local copies, waits for them, and re-layouts: 16.9 us -> 1.98 us
  matrix products: 13.5 us -> 0 us
    pallas_call x0 -> x5, Pallas kernels: none -> 126 us  [the longest x2 112 us: exchange(): pl.pallas_call(functools.partial(exchange_kernel, orders), out_shape=[sha...]
    all_to_all x7 -> x0, waiting for transfers between devices: 109 us -> none  [the longest x1 18.6 us: shards(): lax.all_to_all(split_cols(arrived[0]), 'ulysses', split_axis=1, concat_ax...]
    all_to_all x7 -> x0, starting transfers between devices: 63.7 us -> none  [the longest x1 22.1 us: shards(): lax.all_to_all(to_slots(keys), 'bag', split_axis=0, concat_axis=0, tiled=...]
    all_to_all x1 -> x0, blocking collectives: 25.4 us -> none  [shards(): lax.all_to_all(attended_bag.reshape(group_count, bag_count * span_len, he...]
    all_to_all x3 -> x0, other arithmetic: 9.44 us -> none  [the longest x1 3.15 us: shards(): lax.all_to_all(to_slots(keys), 'bag', split_axis=0, concat_axis=0, tiled=...]
    unnamed x17 -> x0, local copies, waits for them, and re-layouts: 7.44 us -> none
    sub x2 -> x0, matrix products: 7.05 us -> none  [one_block(): expo = jnp.exp(scores - row_max)]
    dot_general x2 -> x0, matrix products: 6.41 us -> none  [one_block(): jnp.einsum('hqk,khd->qhd', weights, value_heads, preferred_element_type=j...]
  transfers between devices with their start and end apart: 7 -> 0, of which waited for: 7 -> 0; matrix products, arithmetic and copies ran while one was open for 8% -> 0% of each run, Pallas kernels for 0% -> 0%
where the time goes in v1:
time: 128 us
  Pallas kernels  126 us (98%)
  local copies, waits for them, and re-layouts  1.98 us (2%)
    pallas_call x2, Pallas kernels, exchange(): pl.pallas_call(functools.partial(exchange_kernel, orders), out_shape=[sha...  112 us
    pallas_call x1, Pallas kernels, shards(): pl.pallas_call(attend_kernel, out_shape=rows, in_specs=[SMEM] + [VMEM] *...  8.87 us
    pallas_call x1, Pallas kernels, shards(): pl.pallas_call(pack_kernel, out_shape=[rows] * 3, in_specs=[VMEM] * 4, ou...  2.85 us

profile of v1, /device:TPU:1, one launch (start us, length us, event | category | flops | bytes accessed | tf_op | source)
XLA Modules:
  0.0 127.7 jit_solution(17987604076958992625)
XLA Ops:
  0.0 1.3 fusion
  1.3 2.8 %pack.1 = (bf16[2048,128]{1,0:T(8,128)(2,1)}, bf16[2048,128]{1,0:T(8,128)(2,1)}, bf16[2048,128]{1,0:T(8,128)(2,1)}) custom-call(s32[1,64]{1,0:T(1,128)} %get-tuple-element.17.route_ref, bf16[64,4096]{1,0:T(8,128)(2,1)} %refs_0_.1, bf16[64,4096]{1,0:T(8,128)(2,1)} %refs_1_.1, bf16[64,4096]{1,0:T(8,128)(2,1)} %refs_2_.1), custom_call_target="tpu_custom_call" | custom-call | tf_op jit(solution)/shard_map/pack/pallas_call | solution.py:179
  4.1 64.3 %exchange_xyz_yzx_zxy.1 = (bf16[8,8,16,2,128]{4,3,2,1,0:T(2,128)(2,1)}, bf16[8,8,16,2,128]{4,3,2,1,0:T(2,128)(2,1)}, bf16[8,8,16,2,128]{4,3,2,1,0:T(2,128)(2,1)}) custom-call(bf16[8,8,16,2,128]{4,3,2,1,0:T(2,128)(2,1)} %bitcast.14, bf16[8,8,16,2,128]{4,3,2,1,0:T(2,128)(2,1)} %bitcast.15, bf16[8,8,16,2,128]{4,3,2,1,0:T(2,128)(2,1)} %bitcast.16), custom_call_target="tpu_custom_call" | custom-call | tf_op jit(solution)/shard_map/exchange_xyz_yzx_zxy/pallas_call | solution.py:126
  68.4 8.9 %attend.1 = bf16[2048,128]{1,0:T(8,128)(2,1)} custom-call(s32[1,4]{1,0:T(1,128)} %len_ref.1, bf16[2048,128]{1,0:T(8,128)(2,1)} %bitcast.17, bf16[2048,128]{1,0:T(8,128)(2,1)} %bitcast.18, bf16[2048,128]{1,0:T(8,128)(2,1)} %bitcast.19), custom_call_target="tpu_custom_call" | custom-call | tf_op jit(solution)/shard_map/attend/pallas_call | solution.py:184
  77.3 47.5 %exchange_xyz.1 = bf16[8,8,16,2,128]{4,3,2,1,0:T(2,128)(2,1)} custom-call(bf16[8,8,16,2,128]{4,3,2,1,0:T(2,128)(2,1)} %bitcast.12), custom_call_target="tpu_custom_call" | custom-call | tf_op jit(solution)/shard_map/exchange_xyz/pallas_call | solution.py:126
  124.8 0.7 copy.6.route_ref
  125.5 2.2 %unpack.1 = bf16[64,4096]{1,0:T(8,128)(2,1)} custom-call(s32[64,1]{1,0:T(8,128)} %copy.6.route_ref, bf16[2048,128]{1,0:T(8,128)(2,1)} %bitcast.13), custom_call_target="tpu_custom_call" | custom-call | tf_op jit(solution)/shard_map/unpack/pallas_call | solution.py:193

commit v2 on v1

v2 whole, which is shorter than its diff:
```python
import math

import jax
import jax.numpy as jnp
from jax import lax
from jax.experimental import pallas as pl
from jax.experimental.pallas import tpu as pltpu
from jax.sharding import PartitionSpec as P

HEADS = 32
HDIM = 128
NX, NY, NZ = 8, 8, 16
TOK = NX * NY * NZ
BIG = 1e30
UNIT = (2, HDIM)
BLOCK = (NX, NY, NZ) + UNIT
MESH = pl.DeviceIdType.MESH
VMEM = pl.BlockSpec(memory_space=pltpu.VMEM)
SMEM = pl.BlockSpec(memory_space=pltpu.SMEM)


def pick_rows(route):
    lane_route = jnp.concatenate([route, route], axis=1)
    row = lax.broadcasted_iota(jnp.int32, (128, 128), 0)
    lane = lax.broadcasted_iota(jnp.int32, (128, 128), 1)
    return ((lane_route == row // 2) & (lane // 64 == row % 2)).astype(jnp.float32)


def place():
    b = lax.axis_index("bag")
    u = lax.axis_index("ulysses")
    return {"x": u // 2, "y": (u % 2) * 4 + b // 16, "z": b % 16}


def device(here, axis, t):
    at = dict(here)
    at[axis] = t
    return ((at["y"] % 4) * 16 + at["z"], at["x"] * 2 + at["y"] // 4)


def slot(ref, axis, t):
    if axis == "x":
        return ref.at[t]
    if axis == "y":
        return ref.at[:, t]
    return ref.at[:, :, t]


SIZE = {"x": NX, "y": NY, "z": NZ}
STEPS = {"x": (4, 3, 5, 2, 6, 1, 7), "y": (4, 3, 5, 2, 6, 1, 7)}
STEPS["z"] = (8, 9, 7, 6, 10, 5, 11, 4, 12, 3, 13, 2, 14, 1, 15)
ORDERS = ("xyz", "yzx", "zxy")


def send_slots(axis, here, src, dst, send, recv, own):
    mine = here[axis]
    for step in STEPS[axis]:
        t = (mine + step) % SIZE[axis]
        pltpu.make_async_remote_copy(
            src_ref=slot(src, axis, t),
            dst_ref=slot(dst, axis, mine),
            send_sem=send,
            recv_sem=recv,
            device_id=device(here, axis, t),
            device_id_type=MESH,
        ).start()
    pltpu.make_async_copy(slot(src, axis, mine), slot(dst, axis, mine), own).start()


def wait_slots(axis, here, src, dst, send, recv, own):
    mine = here[axis]
    part = slot(dst, axis, pl.ds(0, SIZE[axis] - 1))
    pltpu.make_async_copy(part, part, recv).wait()
    pltpu.make_async_copy(part, part, send).wait()
    pltpu.make_async_copy(slot(src, axis, mine), slot(dst, axis, mine), own).wait()


def main_kernel(
    len_ref, route_ref, q_ref, k_ref, v_ref, back,
    units, mid1, mid2, fin, wide, out_rows, q_seq, k_seq, o_units, ret1, ret2,
    send, recv, own, rsend, xrecv, yrecv, yown, zrecv, zown,
):
    here = place()
    barrier = pltpu.get_barrier_semaphore()
    for axis in "xyz":
        for step in STEPS[axis]:
            t = (here[axis] + step) % SIZE[axis]
            pl.semaphore_signal(
                barrier, inc=1, device_id=device(here, axis, t), device_id_type=MESH
            )

    pick = pick_rows(route_ref[pl.ds(lax.axis_index("ulysses"), 1), :]).astype(jnp.bfloat16)
    bufs = (units, mid1, mid2, fin)

    def args(i, stage):
        return (
            ORDERS[i][stage], here, bufs[stage].at[i], bufs[stage + 1].at[i],
            send.at[i, stage], recv.at[i, stage], own.at[i, stage],
        )

    for i, in_ref in enumerate((q_ref, k_ref, v_ref)):
        flat = units.at[i].reshape(2 * TOK, HDIM)
        for u in range(16):
            pair = jnp.concatenate(
                [in_ref[:, u * 256 : u * 256 + 128], in_ref[:, u * 256 + 128 : u * 256 + 256]],
                axis=0,
            )
            rows = jnp.dot(pick, pair, preferred_element_type=jnp.float32)
            flat[u * 128 : (u + 1) * 128, :] = rows.astype(jnp.bfloat16)
        if i == 0:
            pl.semaphore_wait(barrier, sum(len(steps) for steps in STEPS.values()))
        send_slots(*args(i, 0))

    pos = lax.broadcasted_iota(jnp.int32, (TOK, HDIM), 0)
    lane = lax.broadcasted_iota(jnp.int32, (TOK, HDIM), 1)
    first = 0
    inside = jnp.zeros((TOK, HDIM), jnp.bool_)
    for e in range(4):
        last = first + len_ref[0, e]
        inside = inside | ((lane == e) & (pos >= first) & (pos < last))
        first = last
    q_seq[...] = jnp.where(inside, 1.0, 0.0).astype(jnp.bfloat16)
    k_seq[...] = jnp.where(inside | (lane >= 4), 0.0, -BIG).astype(jnp.bfloat16)

    for stage in (1, 2):
        for i in range(3):
            wait_slots(*args(i, stage - 1))
            send_slots(*args(i, stage))
    for i in (1, 2, 0):
        wait_slots(*args(i, 2))
        wide[i] = fin.at[i].reshape(2 * TOK, HDIM)[...].astype(jnp.float32)

    x = here["x"]
    factor = math.log2(math.e) / math.sqrt(HDIM)
    flat_out = o_units.reshape(2 * TOK, HDIM)
    heads = []
    for h in range(2):
        keys = wide[1, pl.ds(h, TOK, stride=2), :].astype(jnp.bfloat16)
        values = wide[2, pl.ds(h, TOK, stride=2), :].astype(jnp.bfloat16)
        heads.append((jnp.concatenate([keys, k_seq[...]], axis=1), values))

    def pair_of(i):
        return (x // 2 + 1 + i) % 4

    def came_from(i):
        return (x // 2 + 3 - i) % 4

    def attend(i):
        j = pair_of(i)
        for h, (keys, values) in enumerate(heads):
            q = wide[0, pl.ds(j * 512 + h, 256, stride=2), :].astype(jnp.bfloat16)
            q = jnp.concatenate([q, q_seq[pl.ds(pl.multiple_of(j * 256, 256), 256), :]], axis=1)
            s = lax.dot_general(
                q, keys, (((1,), (1,)), ((), ())), preferred_element_type=jnp.float32
            )
            e = jnp.exp2((s - jnp.max(s, axis=1, keepdims=True)) * factor)
            w = (e * (1.0 / jnp.sum(e, axis=1, keepdims=True))).astype(jnp.bfloat16)
            out_rows[pl.ds(h, 256, stride=2), :] = jnp.dot(
                w, values, preferred_element_type=jnp.float32
            )
        flat_out[pl.ds(pl.multiple_of(j * 512, 512), 512), :] = out_rows[...].astype(jnp.bfloat16)

    def send_x(t):
        pltpu.make_async_remote_copy(
            src_ref=o_units.at[t],
            dst_ref=ret1.at[x],
            send_sem=rsend.at[0],
            recv_sem=xrecv.at[x],
            device_id=device(here, "x", t),
            device_id_type=MESH,
        ).start()

    def forward_y(i):
        j = came_from(i)
        for r in range(2):
            piece = ret1.at[j * 2 + r]
            pltpu.make_async_copy(piece, piece, xrecv.at[j * 2 + r]).wait()
        both = pl.ds(j * 2, 2)
        for step in STEPS["y"]:
            t = (here["y"] + step) % NY
            pltpu.make_async_remote_copy(
                src_ref=ret1.at[both, t],
                dst_ref=ret2.at[both, here["y"]],
                send_sem=rsend.at[1],
                recv_sem=yrecv.at[j],
                device_id=device(here, "y", t),
                device_id_type=MESH,
            ).start()
        pltpu.make_async_copy(
            ret1.at[both, here["y"]], ret2.at[both, here["y"]], yown.at[j]
        ).start()

    def forward_z(i):
        j = came_from(i)
        both = pl.ds(j * 2, 2)
        most = ret2.at[both, pl.ds(0, NY - 1)]
        pltpu.make_async_copy(most, most, yrecv.at[j]).wait()
        pltpu.make_async_copy(
            ret1.at[both, here["y"]], ret2.at[both, here["y"]], yown.at[j]
        ).wait()
        for step in STEPS["z"]:
            t = (here["z"] + step) % NZ
            pltpu.make_async_remote_copy(
                src_ref=ret2.at[both, :, t],
                dst_ref=back.at[both, :, here["z"]],
                send_sem=rsend.at[2],
                recv_sem=zrecv,
                device_id=device(here, "z", t),
                device_id_type=MESH,
            ).start()
        pltpu.make_async_copy(
            ret2.at[both, :, here["z"]], back.at[both, :, here["z"]], zown.at[j]
        ).start()

    def block(i, _):
        attend(i)

        @pl.when(i < 3)
        def _():
            send_x(pair_of(i) * 2)
            send_x(pair_of(i) * 2 + 1)

        @pl.when(i == 3)
        def _():
            send_x(x // 2 * 2 + 1 - x % 2)
            pltpu.make_async_copy(o_units.at[x], ret1.at[x], xrecv.at[x]).start()

        @pl.when(i >= 2)
        def _():
            forward_y(i - 2)

        return 0

    lax.fori_loop(0, 4, block, 0)
    lax.fori_loop(2, 4, lambda i, _: (forward_y(i), 0)[1], 0)
    lax.fori_loop(0, 4, lambda i, _: (forward_z(i), 0)[1], 0)

    for i in range(4):
        j = came_from(i)
        mine = here["z"]
        pltpu.make_async_copy(
            ret2.at[pl.ds(j * 2, 2), :, mine], back.at[pl.ds(j * 2, 2), :, mine], zown.at[j]
        ).wait()
    for n, axis in enumerate("xyz"):
        part = slot(back, axis, pl.ds(0, SIZE[axis] - 1))
        if axis == "z":
            pltpu.make_async_copy(part, part, zrecv).wait()
        pltpu.make_async_copy(part, part, rsend.at[n]).wait()


def unpack_kernel(route_ref, i_ref, o_ref):
    pick = pick_rows(route_ref[pl.ds(lax.axis_index("ulysses"), 1), :]).T.astype(jnp.bfloat16)
    for u in range(16):
        both = jnp.dot(
            pick, i_ref[u * 128 : (u + 1) * 128, :], preferred_element_type=jnp.float32
        ).astype(jnp.bfloat16)
        o_ref[:, u * 256 : u * 256 + 128] = both[:64]
        o_ref[:, u * 256 + 128 : u * 256 + 256] = both[64:]


def shards(queries, keys, values, span_route, seq_lengths):
    route = span_route[0]
    block = pltpu.VMEM(BLOCK, jnp.bfloat16)
    three = pltpu.VMEM((3,) + BLOCK, jnp.bfloat16)
    dma = pltpu.SemaphoreType.DMA
    back = pl.pallas_call(
        main_kernel,
        out_shape=jax.ShapeDtypeStruct(BLOCK, jnp.bfloat16),
        in_specs=[SMEM] + [VMEM] * 4,
        out_specs=VMEM,
        scratch_shapes=[three] * 4
        + [
            pltpu.VMEM((3, 2 * TOK, HDIM), jnp.float32),
            pltpu.VMEM((512, HDIM), jnp.float32),
            pltpu.VMEM((TOK, HDIM), jnp.bfloat16),
            pltpu.VMEM((TOK, HDIM), jnp.bfloat16),
            block, block, block,
            dma((3, 3)), dma((3, 3)), dma((3, 3)),
            dma((3,)), dma((NX,)), dma((4,)), dma((4,)), dma, dma((4,)),
        ],
        compiler_params=pltpu.CompilerParams(has_side_effects=True, collective_id=1),
        name="dispatch_attend_return",
    )(seq_lengths, route, queries, keys, values)
    return pl.pallas_call(
        unpack_kernel,
        out_shape=jax.ShapeDtypeStruct(queries.shape, jnp.bfloat16),
        in_specs=[VMEM] * 2,
        out_specs=VMEM,
        name="unpack",
    )(route, back.reshape(2 * TOK, HDIM))


def solution(mesh):
    placed = (
        P(("bag", "ulysses"), None),
        P(("bag", "ulysses"), None),
        P(("bag", "ulysses"), None),
        P("bag", None, None),
        P("bag", None),
    )
    return jax.shard_map(
        shards, mesh=mesh, in_specs=placed, out_specs=P(("bag", "ulysses"), None), check_vma=False
    )
```

time: 128 us -> 100 us (0.78)
  Pallas kernels: 126 us -> 100 us
  local copies, waits for them, and re-layouts: 1.98 us -> 0 us
    pallas_call x4 -> x1, Pallas kernels: 124 us -> 98 us  [shards(): pl.pallas_call(main_kernel, out_shape=jax.ShapeDtypeStruct(BLOCK, jnp.bfl...]
where the time goes in v2:
time: 100 us
  Pallas kernels  100 us (100%)
    pallas_call x1, Pallas kernels, shards(): pl.pallas_call(main_kernel, out_shape=jax.ShapeDtypeStruct(BLOCK, jnp.bfl...  98 us
    pallas_call x1, Pallas kernels, shards(): pl.pallas_call(unpack_kernel, out_shape=jax.ShapeDtypeStruct(queries.shap...  2.29 us

profile of v2, /device:TPU:1, one launch (start us, length us, event | category | flops | bytes accessed | tf_op | source)
XLA Modules:
  0.0 100.3 jit_solution(17351769491390034442)
XLA Ops:
  0.0 98.0 %dispatch_attend_return.1 = bf16[8,8,16,2,128]{4,3,2,1,0:T(2,128)(2,1)} custom-call(s32[1,4]{1,0:T(1,128)} %len_ref.1, s32[16,64]{1,0:T(8,128)} %bitcast.3, bf16[64,4096]{1,0:T(8,128)(2,1)} %q_ref.1, bf16[64,4096]{1,0:T(8,128)(2,1)} %k_ref.1, bf16[64,4096]{1,0:T(8,128)(2,1)} %v_ref.1), custom_call_target="tpu_custom_call" | custom-call | tf_op jit(solution)/shard_map/dispatch_attend_return/pallas_call | solution.py:266
  98.0 2.3 %unpack.1 = bf16[64,4096]{1,0:T(8,128)(2,1)} custom-call(s32[16,64]{1,0:T(8,128)} %bitcast.4, bf16[2048,128]{1,0:T(8,128)(2,1)} %bitcast.2), custom_call_target="tpu_custom_call" | custom-call | tf_op jit(solution)/shard_map/unpack/pallas_call | solution.py:284

commit v3 on v2

v3 whole, which is shorter than its diff:
```python
import math

import jax
import jax.numpy as jnp
from jax import lax
from jax.experimental import pallas as pl
from jax.experimental.pallas import tpu as pltpu
from jax.sharding import PartitionSpec as P

HEADS = 32
HDIM = 128
NX, NY, NZ = 8, 8, 16
TOK = NX * NY * NZ
BIG = 1e30
UNIT = (2, HDIM)
BLOCK = (NX, NY, NZ) + UNIT
MESH = pl.DeviceIdType.MESH
VMEM = pl.BlockSpec(memory_space=pltpu.VMEM)
SMEM = pl.BlockSpec(memory_space=pltpu.SMEM)


def pick_rows(route):
    lane_route = jnp.concatenate([route, route], axis=1)
    row = lax.broadcasted_iota(jnp.int32, (128, 128), 0)
    lane = lax.broadcasted_iota(jnp.int32, (128, 128), 1)
    return ((lane_route == row // 2) & (lane // 64 == row % 2)).astype(jnp.float32)


def place():
    b = lax.axis_index("bag")
    u = lax.axis_index("ulysses")
    return {"x": u // 2, "y": (u % 2) * 4 + b // 16, "z": b % 16}


def device(here, axis, t):
    at = dict(here)
    at[axis] = t
    return ((at["y"] % 4) * 16 + at["z"], at["x"] * 2 + at["y"] // 4)


def view(ref, **at):
    return ref.at[tuple(at.get(axis, slice(None)) for axis in "xyz")]


SIZE = {"x": NX, "y": NY, "z": NZ}
STEPS = {"x": (4, 3, 5, 2, 6, 1, 7), "y": (4, 3, 5, 2, 6, 1, 7)}
STEPS["z"] = (8, 9, 7, 6, 10, 5, 11, 4, 12, 3, 13, 2, 14, 1, 15)
ORDERS = ("xyz", "yzx", "zxy")
PARTS = ("xyz", "yzx", "zxy", "zxy")
GROUPS = 4
OFFSETS = (2, 1, 3, 0)


def send_to(here, axis, t, src, dst, send, recv):
    pltpu.make_async_remote_copy(
        src_ref=src,
        dst_ref=dst,
        send_sem=send,
        recv_sem=recv,
        device_id=device(here, axis, t),
        device_id_type=MESH,
    ).start()


def wait_for(ref, sem):
    pltpu.make_async_copy(ref, ref, sem).wait()


def main_kernel(
    len_ref, route_ref, q_ref, k_ref, v_ref, back,
    units, mid1, mid2, fin, wide, out_rows, q_seq, k_seq, o_units, ret1, ret2, ret3,
    send, recv1, recv2, recv3, own1, own2, own3, rsend, rrecv, rown,
):
    here = place()
    barrier = pltpu.get_barrier_semaphore()
    for axis in "xyz":
        for step in STEPS[axis]:
            t = (here[axis] + step) % SIZE[axis]
            pl.semaphore_signal(
                barrier, inc=1, device_id=device(here, axis, t), device_id_type=MESH
            )

    pick = pick_rows(route_ref[pl.ds(lax.axis_index("ulysses"), 1), :]).astype(jnp.bfloat16)

    def whole(axis):
        return view(fin.at[0], **{axis: pl.ds(0, SIZE[axis] - 1)})

    def group(i, off):
        axis = ORDERS[i][0]
        width = SIZE[axis] // GROUPS
        j = (here[axis] // width + GROUPS - off) % GROUPS
        return axis, width, j, pl.ds(j * width, width)

    def send1(i):
        axis = ORDERS[i][0]
        mine, width = here[axis], SIZE[axis] // GROUPS
        at_mine = {axis: mine}
        for off in OFFSETS:
            j = (mine // width + off) % GROUPS
            for r in range(0 if off else 1, width):
                t = j * width + (r if off else (mine + r) % width)
                send_to(
                    here, axis, t, view(units.at[i], **{axis: t}), view(mid1.at[i], **at_mine),
                    send.at[i, 0], recv1.at[i, mine // width],
                )
        copy1(i).start()

    def copy1(i):
        at_mine = {ORDERS[i][0]: here[ORDERS[i][0]]}
        return pltpu.make_async_copy(
            view(units.at[i], **at_mine), view(mid1.at[i], **at_mine), own1.at[i]
        )

    def send2(i, off):
        first, width, j, rows = group(i, off)
        axis = ORDERS[i][1]
        if off:
            wait_for(view(mid1.at[i], **{first: rows}), recv1.at[i, j])
        else:
            wait_for(view(mid1.at[i], **{first: pl.ds(0, width - 1)}), recv1.at[i, j])
            copy1(i).wait()
        for step in STEPS[axis]:
            t = (here[axis] + step) % SIZE[axis]
            send_to(
                here, axis, t, view(mid1.at[i], **{first: rows, axis: t}),
                view(mid2.at[i], **{first: rows, axis: here[axis]}), send.at[i, 1], recv2.at[i, j],
            )
        copy2(i, off).start()

    def copy2(i, off):
        first, _, j, rows = group(i, off)
        at = {first: rows, ORDERS[i][1]: here[ORDERS[i][1]]}
        return pltpu.make_async_copy(view(mid1.at[i], **at), view(mid2.at[i], **at), own2.at[i, j])

    def send3(i, off):
        first, _, j, rows = group(i, off)
        second, axis = ORDERS[i][1:]
        wait_for(view(mid2.at[i], **{first: rows, second: pl.ds(0, SIZE[second] - 1)}), recv2.at[i, j])
        copy2(i, off).wait()
        for step in STEPS[axis]:
            t = (here[axis] + step) % SIZE[axis]
            send_to(
                here, axis, t, view(mid2.at[i], **{first: rows, axis: t}),
                view(fin.at[i], **{first: rows, axis: here[axis]}), send.at[i, 2], recv3.at[i],
            )
        copy3(i, off).start()

    def copy3(i, off):
        first, _, j, rows = group(i, off)
        at = {first: rows, ORDERS[i][2]: here[ORDERS[i][2]]}
        return pltpu.make_async_copy(view(mid2.at[i], **at), view(fin.at[i], **at), own3.at[i, j])

    for i, in_ref in enumerate((q_ref, k_ref, v_ref)):
        flat = units.at[i].reshape(2 * TOK, HDIM)
        for u in range(16):
            pair = jnp.concatenate(
                [in_ref[:, u * 256 : u * 256 + 128], in_ref[:, u * 256 + 128 : u * 256 + 256]],
                axis=0,
            )
            rows = jnp.dot(pick, pair, preferred_element_type=jnp.float32)
            flat[u * 128 : (u + 1) * 128, :] = rows.astype(jnp.bfloat16)
        if i == 0:
            pl.semaphore_wait(barrier, sum(len(steps) for steps in STEPS.values()))
        send1(i)

    pos = lax.broadcasted_iota(jnp.int32, (TOK, HDIM), 0)
    lane = lax.broadcasted_iota(jnp.int32, (TOK, HDIM), 1)
    first = 0
    inside = jnp.zeros((TOK, HDIM), jnp.bool_)
    for e in range(4):
        last = first + len_ref[0, e]
        inside = inside | ((lane == e) & (pos >= first) & (pos < last))
        first = last
    q_seq[...] = jnp.where(inside, 1.0, 0.0).astype(jnp.bfloat16)
    k_seq[...] = jnp.where(inside | (lane >= 4), 0.0, -BIG).astype(jnp.bfloat16)

    for send_on in (send2, send3):
        for off in OFFSETS:
            for i in range(3):
                send_on(i, off)
    for i in (1, 2, 0):
        wait_for(whole(ORDERS[i][2]), recv3.at[i])
        for off in OFFSETS:
            copy3(i, off).wait()
        wide[i] = fin.at[i].reshape(2 * TOK, HDIM)[...].astype(jnp.float32)

    x = here["x"]
    factor = math.log2(math.e) / math.sqrt(HDIM)
    flat_out = o_units.reshape(2 * TOK, HDIM)
    heads = []
    for h in range(2):
        keys = wide[1, pl.ds(h, TOK, stride=2), :].astype(jnp.bfloat16)
        values = wide[2, pl.ds(h, TOK, stride=2), :].astype(jnp.bfloat16)
        heads.append((jnp.concatenate([keys, k_seq[...]], axis=1), values))

    def pair_of(i):
        return (x // 2 + 6 - i) % 4

    def attend(i):
        j = pair_of(i)
        for h, (keys, values) in enumerate(heads):
            q = wide[0, pl.ds(j * 512 + h, 256, stride=2), :].astype(jnp.bfloat16)
            q = jnp.concatenate([q, q_seq[pl.ds(pl.multiple_of(j * 256, 256), 256), :]], axis=1)
            s = lax.dot_general(
                q, keys, (((1,), (1,)), ((), ())), preferred_element_type=jnp.float32
            )
            e = jnp.exp2((s - jnp.max(s, axis=1, keepdims=True)) * factor)
            w = (e * (1.0 / jnp.sum(e, axis=1, keepdims=True))).astype(jnp.bfloat16)
            out_rows[pl.ds(h, 256, stride=2), :] = jnp.dot(
                w, values, preferred_element_type=jnp.float32
            )
        flat_out[pl.ds(pl.multiple_of(j * 512, 512), 512), :] = out_rows[...].astype(jnp.bfloat16)

    stops = (
        (o_units, ret1, ret2, back),
        (o_units, ret1, ret2, back),
        (o_units, ret1, ret3, back),
        (o_units, ret1, ret3, back),
    )

    def rows_at(p, stage):
        j = pair_of(p) if "x" not in PARTS[p][:stage] else (x // 2 + 2 + p) % 4
        return pl.ds(j * 2, 2)

    def back_copy(p, stage):
        axis = PARTS[p][stage]
        at = {"x": rows_at(p, stage)}
        at[axis] = here[axis]
        src, dst = stops[p][stage : stage + 2]
        return pltpu.make_async_copy(view(src, **at), view(dst, **at), rown.at[p, stage])

    def back_send(p, stage):
        axis = PARTS[p][stage]
        src, dst = stops[p][stage : stage + 2]
        sems = (rsend.at[p, stage], rrecv.at[p, stage])
        if axis == "x":
            targets = [pair_of(p) * 2, pair_of(p) * 2 + 1] if p != 2 else [x // 2 * 2 + 1 - x % 2]
            for t in targets:
                send_to(here, "x", t, view(src, x=t), view(dst, x=x), *sems)
        else:
            rows = rows_at(p, stage)
            for step in STEPS[axis]:
                t = (here[axis] + step) % SIZE[axis]
                send_to(
                    here, axis, t, view(src, **{"x": rows, axis: t}),
                    view(dst, **{"x": rows, axis: here[axis]}), *sems,
                )
        if axis != "x" or p == 2:
            back_copy(p, stage).start()

    def back_bytes(p, stage):
        axis = PARTS[p][stage]
        if axis == "x":
            return view(back, x=pl.ds(0, 1 if p == 2 else 2))
        return view(back, **{"x": pl.ds(0, 2), axis: pl.ds(0, SIZE[axis] - 1)})

    def back_wait(p, stage):
        wait_for(back_bytes(p, stage), rrecv.at[p, stage])
        if PARTS[p][stage] != "x" or p == 2:
            back_copy(p, stage).wait()

    def block(i, _):
        attend(i)
        for p in range(4):

            @pl.when(i == p)
            def _(p=p):
                back_send(p, 0)

        return 0

    lax.fori_loop(0, 4, block, 0)
    for stage in (1, 2):
        for p in range(4):
            back_wait(p, stage - 1)
            back_send(p, stage)
    for p in range(4):
        back_wait(p, 2)
    for p in range(4):
        for stage in range(3):
            wait_for(back_bytes(p, stage), rsend.at[p, stage])
    for i in range(3):
        for stage in range(3):
            wait_for(whole(ORDERS[i][stage]), send.at[i, stage])


def unpack_kernel(route_ref, i_ref, o_ref):
    pick = pick_rows(route_ref[pl.ds(lax.axis_index("ulysses"), 1), :]).T.astype(jnp.bfloat16)
    for u in range(16):
        both = jnp.dot(
            pick, i_ref[u * 128 : (u + 1) * 128, :], preferred_element_type=jnp.float32
        ).astype(jnp.bfloat16)
        o_ref[:, u * 256 : u * 256 + 128] = both[:64]
        o_ref[:, u * 256 + 128 : u * 256 + 256] = both[64:]


def shards(queries, keys, values, span_route, seq_lengths):
    route = span_route[0]
    block = pltpu.VMEM(BLOCK, jnp.bfloat16)
    three = pltpu.VMEM((3,) + BLOCK, jnp.bfloat16)
    dma = pltpu.SemaphoreType.DMA
    back = pl.pallas_call(
        main_kernel,
        out_shape=jax.ShapeDtypeStruct(BLOCK, jnp.bfloat16),
        in_specs=[SMEM] + [VMEM] * 4,
        out_specs=VMEM,
        scratch_shapes=[three] * 4
        + [
            pltpu.VMEM((3, 2 * TOK, HDIM), jnp.float32),
            pltpu.VMEM((512, HDIM), jnp.float32),
            pltpu.VMEM((TOK, HDIM), jnp.bfloat16),
            pltpu.VMEM((TOK, HDIM), jnp.bfloat16),
            block, block, block, block,
            dma((3, 3)), dma((3, 4)), dma((3, 4)), dma((3,)), dma((3,)), dma((3, 4)), dma((3, 4)),
            dma((4, 3)), dma((4, 3)), dma((4, 3)),
        ],
        compiler_params=pltpu.CompilerParams(has_side_effects=True, collective_id=1),
        name="dispatch_attend_return",
    )(seq_lengths, route, queries, keys, values)
    return pl.pallas_call(
        unpack_kernel,
        out_shape=jax.ShapeDtypeStruct(queries.shape, jnp.bfloat16),
        in_specs=[VMEM] * 2,
        out_specs=VMEM,
        name="unpack",
    )(route, back.reshape(2 * TOK, HDIM))


def solution(mesh):
    placed = (
        P(("bag", "ulysses"), None),
        P(("bag", "ulysses"), None),
        P(("bag", "ulysses"), None),
        P("bag", None, None),
        P("bag", None),
    )
    return jax.shard_map(
        shards, mesh=mesh, in_specs=placed, out_specs=P(("bag", "ulysses"), None), check_vma=False
    )
```

time: 100 us -> 92.5 us (0.925); the launches traced: 100 us -> 90.9 us
  Pallas kernels: 100 us -> 90.9 us
    pallas_call x1, Pallas kernels: 98 us -> 88.6 us  [shards(): pl.pallas_call(main_kernel, out_shape=jax.ShapeDtypeStruct(BLOCK, jnp.bfl...]
where the time goes in v3:
time: 92.5 us; the launch traced here: 90.9 us
  Pallas kernels  90.9 us (98%)
    pallas_call x1, Pallas kernels, shards(): pl.pallas_call(main_kernel, out_shape=jax.ShapeDtypeStruct(BLOCK, jnp.bfl...  88.6 us
    pallas_call x1, Pallas kernels, shards(): pl.pallas_call(unpack_kernel, out_shape=jax.ShapeDtypeStruct(queries.shap...  2.3 us

profile of v3, /device:TPU:1, one launch (start us, length us, event | category | flops | bytes accessed | tf_op | source)
XLA Modules:
  0.0 90.9 jit_solution(14138552687293493667)
XLA Ops:
  0.0 88.6 %dispatch_attend_return.1 = bf16[8,8,16,2,128]{4,3,2,1,0:T(2,128)(2,1)} custom-call(s32[1,4]{1,0:T(1,128)} %len_ref.1, s32[16,64]{1,0:T(8,128)} %bitcast.3, bf16[64,4096]{1,0:T(8,128)(2,1)} %q_ref.1, bf16[64,4096]{1,0:T(8,128)(2,1)} %k_ref.1, bf16[64,4096]{1,0:T(8,128)(2,1)} %v_ref.1), custom_call_target="tpu_custom_call" | custom-call | tf_op jit(solution)/shard_map/dispatch_attend_return/pallas_call | solution.py:302
  88.6 2.3 %unpack.1 = bf16[64,4096]{1,0:T(8,128)(2,1)} custom-call(s32[16,64]{1,0:T(8,128)} %bitcast.4, bf16[2048,128]{1,0:T(8,128)(2,1)} %bitcast.2), custom_call_target="tpu_custom_call" | custom-call | tf_op jit(solution)/shard_map/unpack/pallas_call | solution.py:320

commit v4 on v3

--- a/solution.py
+++ b/solution.py
@@ -26,16 +26,24 @@
     return ((lane_route == row // 2) & (lane // 64 == row % 2)).astype(jnp.float32)
 
 
+def div(a, n):
+    return lax.div(a, jnp.int32(n))
+
+
+def rem(a, n):
+    return lax.rem(a, jnp.int32(n))
+
+
 def place():
     b = lax.axis_index("bag")
     u = lax.axis_index("ulysses")
-    return {"x": u // 2, "y": (u % 2) * 4 + b // 16, "z": b % 16}
+    return {"x": div(u, 2), "y": rem(u, 2) * 4 + div(b, 16), "z": rem(b, 16)}
 
 
 def device(here, axis, t):
     at = dict(here)
     at[axis] = t
-    return ((at["y"] % 4) * 16 + at["z"], at["x"] * 2 + at["y"] // 4)
+    return (rem(at["y"], 4) * 16 + at["z"], at["x"] * 2 + div(at["y"], 4))
 
 
 def view(ref, **at):
@@ -43,12 +51,20 @@
 
 
 SIZE = {"x": NX, "y": NY, "z": NZ}
-STEPS = {"x": (4, 3, 5, 2, 6, 1, 7), "y": (4, 3, 5, 2, 6, 1, 7)}
-STEPS["z"] = (8, 9, 7, 6, 10, 5, 11, 4, 12, 3, 13, 2, 14, 1, 15)
+STEPS = (4, 3, 5, 2, 6, 1, 7)
 ORDERS = ("xyz", "yzx", "zxy")
 PARTS = ("xyz", "yzx", "zxy", "zxy")
 GROUPS = 4
 OFFSETS = (2, 1, 3, 0)
+
+
+def others(here, axis):
+    mine = here[axis]
+    if axis != "z":
+        return [rem(mine + step, 8) for step in STEPS]
+    chip, core = div(mine, 2), rem(mine, 2)
+    chips = [rem(chip + step, 8) * 2 for step in STEPS]
+    return [c + k for c in chips for k in (core, 1 - core)] + [chip * 2 + 1 - core]
 
 
 def send_to(here, axis, t, src, dst, send, recv):
@@ -68,14 +84,20 @@
 
 def main_kernel(
     len_ref, route_ref, q_ref, k_ref, v_ref, back,
-    units, mid1, mid2, fin, wide, out_rows, q_seq, k_seq, o_units, ret1, ret2, ret3,
-    send, recv1, recv2, recv3, own1, own2, own3, rsend, rrecv, rown,
+    tokens, units, mid1, mid2, fin, wide, rows32, q_seq, keys, values, o_units, ret1, ret2, ret3,
+    load, send, recv1, recv2, recv3, own1, own2, own3, rsend, rrecv, rown,
 ):
+    loads = [
+        pltpu.make_async_copy(ref, tokens.at[i], load.at[i])
+        for i, ref in enumerate((q_ref, k_ref, v_ref))
+    ]
+    for copy in loads:
+        copy.start()
     here = place()
     barrier = pltpu.get_barrier_semaphore()
+    peers = {axis: others(here, axis) for axis in "xyz"}
     for axis in "xyz":
-        for step in STEPS[axis]:
-            t = (here[axis] + step) % SIZE[axis]
+        for t in peers[axis]:
             pl.semaphore_signal(
                 barrier, inc=1, device_id=device(here, axis, t), device_id_type=MESH
             )
@@ -88,20 +110,21 @@
     def group(i, off):
         axis = ORDERS[i][0]
         width = SIZE[axis] // GROUPS
-        j = (here[axis] // width + GROUPS - off) % GROUPS
+        j = rem(div(here[axis], width) + GROUPS - off, GROUPS)
         return axis, width, j, pl.ds(j * width, width)
 
     def send1(i):
         axis = ORDERS[i][0]
         mine, width = here[axis], SIZE[axis] // GROUPS
         at_mine = {axis: mine}
+        ours = div(mine, width)
         for off in OFFSETS:
-            j = (mine // width + off) % GROUPS
+            j = rem(ours + off, GROUPS)
             for r in range(0 if off else 1, width):
-                t = j * width + (r if off else (mine + r) % width)
+                t = j * width + (r if off else rem(mine + r, width))
                 send_to(
                     here, axis, t, view(units.at[i], **{axis: t}), view(mid1.at[i], **at_mine),
-                    send.at[i, 0], recv1.at[i, mine // width],
+                    send.at[i, 0], recv1.at[i, ours],
                 )
         copy1(i).start()
 
@@ -119,8 +142,7 @@
         else:
             wait_for(view(mid1.at[i], **{first: pl.ds(0, width - 1)}), recv1.at[i, j])
             copy1(i).wait()
-        for step in STEPS[axis]:
-            t = (here[axis] + step) % SIZE[axis]
+        for t in peers[axis]:
             send_to(
                 here, axis, t, view(mid1.at[i], **{first: rows, axis: t}),
                 view(mid2.at[i], **{first: rows, axis: here[axis]}), send.at[i, 1], recv2.at[i, j],
@@ -137,8 +159,7 @@
         second, axis = ORDERS[i][1:]
         wait_for(view(mid2.at[i], **{first: rows, second: pl.ds(0, SIZE[second] - 1)}), recv2.at[i, j])
         copy2(i, off).wait()
-        for step in STEPS[axis]:
-            t = (here[axis] + step) % SIZE[axis]
+        for t in peers[axis]:
             send_to(
                 here, axis, t, view(mid2.at[i], **{first: rows, axis: t}),
                 view(fin.at[i], **{first: rows, axis: here[axis]}), send.at[i, 2], recv3.at[i],
@@ -150,17 +171,26 @@
         at = {first: rows, ORDERS[i][2]: here[ORDERS[i][2]]}
         return pltpu.make_async_copy(view(mid2.at[i], **at), view(fin.at[i], **at), own3.at[i, j])
 
-    for i, in_ref in enumerate((q_ref, k_ref, v_ref)):
+    for i in range(3):
+        loads[i].wait()
+        in_ref = tokens.at[i]
         flat = units.at[i].reshape(2 * TOK, HDIM)
-        for u in range(16):
-            pair = jnp.concatenate(
-                [in_ref[:, u * 256 : u * 256 + 128], in_ref[:, u * 256 + 128 : u * 256 + 256]],
-                axis=0,
-            )
-            rows = jnp.dot(pick, pair, preferred_element_type=jnp.float32)
-            flat[u * 128 : (u + 1) * 128, :] = rows.astype(jnp.bfloat16)
+        for u in range(0, 16, 2):
+            c = u * 256
+            halves = [
+                jnp.concatenate(
+                    [in_ref[:, c + h * 128 : c + h * 128 + 128],
+                     in_ref[:, c + 256 + h * 128 : c + 384 + h * 128]], axis=1
+                )
+                for h in range(2)
+            ]
+            rows = jnp.dot(
+                pick, jnp.concatenate(halves, axis=0), preferred_element_type=jnp.float32
+            ).astype(jnp.bfloat16)
+            flat[u * 128 : (u + 1) * 128, :] = rows[:, :128]
+            flat[(u + 1) * 128 : (u + 2) * 128, :] = rows[:, 128:]
         if i == 0:
-            pl.semaphore_wait(barrier, sum(len(steps) for steps in STEPS.values()))
+            pl.semaphore_wait(barrier, sum(SIZE.values()) - 3)
         send1(i)
 
     pos = lax.broadcasted_iota(jnp.int32, (TOK, HDIM), 0)
@@ -172,7 +202,9 @@
         inside = inside | ((lane == e) & (pos >= first) & (pos < last))
         first = last
     q_seq[...] = jnp.where(inside, 1.0, 0.0).astype(jnp.bfloat16)
-    k_seq[...] = jnp.where(inside | (lane >= 4), 0.0, -BIG).astype(jnp.bfloat16)
+    outside = jnp.where(inside | (lane >= 4), 0.0, -BIG).astype(jnp.bfloat16)
+    for h in range(2):
+        keys[h, :, HDIM:] = outside
 
     for send_on in (send2, send3):
         for off in OFFSETS:
@@ -182,34 +214,40 @@
         wait_for(whole(ORDERS[i][2]), recv3.at[i])
         for off in OFFSETS:
             copy3(i, off).wait()
-        wide[i] = fin.at[i].reshape(2 * TOK, HDIM)[...].astype(jnp.float32)
+        if i:
+            wide[i - 1] = fin.at[i].reshape(2 * TOK, HDIM)[...].astype(jnp.float32)
+            for h in range(2):
+                head = wide[i - 1, pl.ds(h, TOK, stride=2), :].astype(jnp.bfloat16)
+                if i == 1:
+                    keys[h, :, :HDIM] = head
+                else:
+                    values[h] = head
 
     x = here["x"]
     factor = math.log2(math.e) / math.sqrt(HDIM)
     flat_out = o_units.reshape(2 * TOK, HDIM)
-    heads = []
-    for h in range(2):
-        keys = wide[1, pl.ds(h, TOK, stride=2), :].astype(jnp.bfloat16)
-        values = wide[2, pl.ds(h, TOK, stride=2), :].astype(jnp.bfloat16)
-        heads.append((jnp.concatenate([keys, k_seq[...]], axis=1), values))
+    flat_in = fin.at[0].reshape(2 * TOK, HDIM)
 
     def pair_of(i):
-        return (x // 2 + 6 - i) % 4
+        return rem(div(x, 2) + 6 - i, 4)
 
     def attend(i):
         j = pair_of(i)
-        for h, (keys, values) in enumerate(heads):
-            q = wide[0, pl.ds(j * 512 + h, 256, stride=2), :].astype(jnp.bfloat16)
-            q = jnp.concatenate([q, q_seq[pl.ds(pl.multiple_of(j * 256, 256), 256), :]], axis=1)
+        here_rows = pl.ds(pl.multiple_of(j * 512, 512), 512)
+        rows32[0] = flat_in[here_rows, :].astype(jnp.float32)
+        seq = q_seq[pl.ds(pl.multiple_of(j * 256, 256), 256), :]
+        for h in range(2):
+            q = rows32[0, pl.ds(h, 256, stride=2), :].astype(jnp.bfloat16)
             s = lax.dot_general(
-                q, keys, (((1,), (1,)), ((), ())), preferred_element_type=jnp.float32
+                jnp.concatenate([q, seq], axis=1), keys[h], (((1,), (1,)), ((), ())),
+                preferred_element_type=jnp.float32,
             )
             e = jnp.exp2((s - jnp.max(s, axis=1, keepdims=True)) * factor)
             w = (e * (1.0 / jnp.sum(e, axis=1, keepdims=True))).astype(jnp.bfloat16)
-            out_rows[pl.ds(h, 256, stride=2), :] = jnp.dot(
-                w, values, preferred_element_type=jnp.float32
-            )
-        flat_out[pl.ds(pl.multiple_of(j * 512, 512), 512), :] = out_rows[...].astype(jnp.bfloat16)
+            rows32[1, pl.ds(h, 256, stride=2), :] = jnp.dot(
+                w, values[h], preferred_element_type=jnp.float32
+            )
+        flat_out[here_rows, :] = rows32[1].astype(jnp.bfloat16)
 
     stops = (
         (o_units, ret1, ret2, back),
@@ -219,7 +257,7 @@
     )
 
     def rows_at(p, stage):
-        j = pair_of(p) if "x" not in PARTS[p][:stage] else (x // 2 + 2 + p) % 4
+        j = pair_of(p) if "x" not in PARTS[p][:stage] else rem(div(x, 2) + 2 + p, 4)
         return pl.ds(j * 2, 2)
 
     def back_copy(p, stage):
@@ -234,13 +272,12 @@
         src, dst = stops[p][stage : stage + 2]
         sems = (rsend.at[p, stage], rrecv.at[p, stage])
         if axis == "x":
-            targets = [pair_of(p) * 2, pair_of(p) * 2 + 1] if p != 2 else [x // 2 * 2 + 1 - x % 2]
+            targets = [pair_of(p) * 2, pair_of(p) * 2 + 1] if p != 2 else [x + 1 - rem(x, 2) * 2]
             for t in targets:
                 send_to(here, "x", t, view(src, x=t), view(dst, x=x), *sems)
         else:
             rows = rows_at(p, stage)
-            for step in STEPS[axis]:
-                t = (here[axis] + step) % SIZE[axis]
+            for t in peers[axis]:
                 send_to(
                     here, axis, t, view(src, **{"x": rows, axis: t}),
                     view(dst, **{"x": rows, axis: here[axis]}), *sems,
@@ -286,7 +323,7 @@
 
 def unpack_kernel(route_ref, i_ref, o_ref):
     pick = pick_rows(route_ref[pl.ds(lax.axis_index("ulysses"), 1), :]).T.astype(jnp.bfloat16)
-    for u in range(16):
+    for u in range(4):
         both = jnp.dot(
             pick, i_ref[u * 128 : (u + 1) * 128, :], preferred_element_type=jnp.float32
         ).astype(jnp.bfloat16)
@@ -302,16 +339,18 @@
     back = pl.pallas_call(
         main_kernel,
         out_shape=jax.ShapeDtypeStruct(BLOCK, jnp.bfloat16),
-        in_specs=[SMEM] + [VMEM] * 4,
+        in_specs=[SMEM, VMEM] + [pl.BlockSpec(memory_space=pl.ANY)] * 3,
         out_specs=VMEM,
-        scratch_shapes=[three] * 4
+        scratch_shapes=[pltpu.VMEM((3,) + queries.shape, jnp.bfloat16)]
+        + [three] * 4
         + [
-            pltpu.VMEM((3, 2 * TOK, HDIM), jnp.float32),
-            pltpu.VMEM((512, HDIM), jnp.float32),
+            pltpu.VMEM((2, 2 * TOK, HDIM), jnp.float32),
+            pltpu.VMEM((2, 512, HDIM), jnp.float32),
             pltpu.VMEM((TOK, HDIM), jnp.bfloat16),
-            pltpu.VMEM((TOK, HDIM), jnp.bfloat16),
+            pltpu.VMEM((2, TOK, 2 * HDIM), jnp.bfloat16),
+            pltpu.VMEM((2, TOK, HDIM), jnp.bfloat16),
             block, block, block, block,
-            dma((3, 3)), dma((3, 4)), dma((3, 4)), dma((3,)), dma((3,)), dma((3, 4)), dma((3, 4)),
+            dma((3,)), dma((3, 3)), dma((3, 4)), dma((3, 4)), dma((3,)), dma((3,)), dma((3, 4)), dma((3, 4)),
             dma((4, 3)), dma((4, 3)), dma((4, 3)),
         ],
         compiler_params=pltpu.CompilerParams(has_side_effects=True, collective_id=1),
@@ -320,8 +359,12 @@
     return pl.pallas_call(
         unpack_kernel,
         out_shape=jax.ShapeDtypeStruct(queries.shape, jnp.bfloat16),
-        in_specs=[VMEM] * 2,
-        out_specs=VMEM,
+        grid=(4,),
+        in_specs=[
+            pl.BlockSpec((16, 64), lambda i: (0, 0)),
+            pl.BlockSpec((512, HDIM), lambda i: (i, 0)),
+        ],
+        out_specs=pl.BlockSpec((64, 1024), lambda i: (0, i)),
         name="unpack",
     )(route, back.reshape(2 * TOK, HDIM))
 

time: 92.5 us -> 94.2 us (1.018)
  Pallas kernels: 90.9 us -> 92.8 us
    pallas_call x1, Pallas kernels: 2.3 us -> 3.8 us  [shards(): pl.pallas_call(unpack_kernel, out_shape=jax.ShapeDtypeStruct(queries.shap...]
where the time goes in v4:
time: 94.2 us; the launch traced here: 92.8 us
  Pallas kernels  92.8 us (99%)
    pallas_call x1, Pallas kernels, shards(): pl.pallas_call(main_kernel, out_shape=jax.ShapeDtypeStruct(BLOCK, jnp.bfl...  89 us
    pallas_call x1, Pallas kernels, shards(): pl.pallas_call(unpack_kernel, out_shape=jax.ShapeDtypeStruct(queries.shap...  3.8 us

profile of v4, /device:TPU:1, one launch (start us, length us, event | category | flops | bytes accessed | tf_op | source)
XLA Modules:
  0.0 92.8 jit_solution(1398263887333821894)
XLA Ops:
  0.0 89.0 %dispatch_attend_return.1 = bf16[8,8,16,2,128]{4,3,2,1,0:T(2,128)(2,1)} custom-call(s32[1,4]{1,0:T(1,128)} %len_ref.1, s32[16,64]{1,0:T(8,128)} %bitcast.3, bf16[64,4096]{1,0:T(8,128)(2,1)} %q_ref.1, bf16[64,4096]{1,0:T(8,128)(2,1)} %k_ref.1, bf16[64,4096]{1,0:T(8,128)(2,1)} %v_ref.1), custom_call_target="tpu_custom_call" | custom-call | tf_op jit(solution)/shard_map/dispatch_attend_return/pallas_call | solution.py:339
  89.0 3.8 %unpack.1 = bf16[64,4096]{1,0:T(8,128)(2,1)} custom-call(s32[16,64]{1,0:T(8,128)} %bitcast.4, bf16[2048,128]{1,0:T(8,128)(2,1)} %bitcast.2), custom_call_target="tpu_custom_call" | custom-call | tf_op jit(solution)/shard_map/unpack/pallas_call | solution.py:359

commit v5 on v4

--- a/solution.py
+++ b/solution.py
@@ -53,7 +53,7 @@
 SIZE = {"x": NX, "y": NY, "z": NZ}
 STEPS = (4, 3, 5, 2, 6, 1, 7)
 ORDERS = ("xyz", "yzx", "zxy")
-PARTS = ("xyz", "yzx", "zxy", "zxy")
+PARTS = ("xyz", "yzx", "zxy", "yxz")
 GROUPS = 4
 OFFSETS = (2, 1, 3, 0)
 
@@ -229,7 +229,8 @@
     flat_in = fin.at[0].reshape(2 * TOK, HDIM)
 
     def pair_of(i):
-        return rem(div(x, 2) + 6 - i, 4)
+        late = div(i, 2)
+        return rem(div(x, 2) + (2 - i) * (1 - late) + (9 - i * 3) * late, 4)
 
     def attend(i):
         j = pair_of(i)
@@ -253,11 +254,11 @@
         (o_units, ret1, ret2, back),
         (o_units, ret1, ret2, back),
         (o_units, ret1, ret3, back),
-        (o_units, ret1, ret3, back),
+        (o_units, ret1, ret2, back),
     )
 
     def rows_at(p, stage):
-        j = pair_of(p) if "x" not in PARTS[p][:stage] else rem(div(x, 2) + 2 + p, 4)
+        j = pair_of(p) if "x" not in PARTS[p][:stage] else rem(div(x, 2) + (2, 3, 1, 0)[p], 4)
         return pl.ds(j * 2, 2)
 
     def back_copy(p, stage):
@@ -272,7 +273,7 @@
         src, dst = stops[p][stage : stage + 2]
         sems = (rsend.at[p, stage], rrecv.at[p, stage])
         if axis == "x":
-            targets = [pair_of(p) * 2, pair_of(p) * 2 + 1] if p != 2 else [x + 1 - rem(x, 2) * 2]
+            targets = [pair_of(p) * 2, pair_of(p) * 2 + 1] if p != 3 else [x + 1 - rem(x, 2) * 2]
             for t in targets:
                 send_to(here, "x", t, view(src, x=t), view(dst, x=x), *sems)
         else:
@@ -282,18 +283,18 @@
                     here, axis, t, view(src, **{"x": rows, axis: t}),
                     view(dst, **{"x": rows, axis: here[axis]}), *sems,
                 )
-        if axis != "x" or p == 2:
+        if axis != "x" or p == 3:
             back_copy(p, stage).start()
 
     def back_bytes(p, stage):
         axis = PARTS[p][stage]
         if axis == "x":
-            return view(back, x=pl.ds(0, 1 if p == 2 else 2))
+            return view(back, x=pl.ds(0, 1 if p == 3 else 2))
         return view(back, **{"x": pl.ds(0, 2), axis: pl.ds(0, SIZE[axis] - 1)})
 
     def back_wait(p, stage):
         wait_for(back_bytes(p, stage), rrecv.at[p, stage])
-        if PARTS[p][stage] != "x" or p == 2:
+        if PARTS[p][stage] != "x" or p == 3:
             back_copy(p, stage).wait()
 
     def block(i, _):
@@ -307,8 +308,8 @@
         return 0
 
     lax.fori_loop(0, 4, block, 0)
-    for stage in (1, 2):
-        for p in range(4):
+    for stage, parts in ((1, (0, 1, 2, 3)), (2, (3, 1, 0, 2))):
+        for p in parts:
             back_wait(p, stage - 1)
             back_send(p, stage)
     for p in range(4):
@@ -323,7 +324,7 @@
 
 def unpack_kernel(route_ref, i_ref, o_ref):
     pick = pick_rows(route_ref[pl.ds(lax.axis_index("ulysses"), 1), :]).T.astype(jnp.bfloat16)
-    for u in range(4):
+    for u in range(16):
         both = jnp.dot(
             pick, i_ref[u * 128 : (u + 1) * 128, :], preferred_element_type=jnp.float32
         ).astype(jnp.bfloat16)
@@ -359,12 +360,8 @@
     return pl.pallas_call(
         unpack_kernel,
         out_shape=jax.ShapeDtypeStruct(queries.shape, jnp.bfloat16),
-        grid=(4,),
-        in_specs=[
-            pl.BlockSpec((16, 64), lambda i: (0, 0)),
-            pl.BlockSpec((512, HDIM), lambda i: (i, 0)),
-        ],
-        out_specs=pl.BlockSpec((64, 1024), lambda i: (0, i)),
+        in_specs=[VMEM] * 2,
+        out_specs=VMEM,
         name="unpack",
     )(route, back.reshape(2 * TOK, HDIM))
 

time: 94.2 us -> 92.5 us (0.982); the launches traced: 92.8 us -> 92.3 us
    pallas_call x1, Pallas kernels: 3.8 us -> 2.3 us  [shards(): pl.pallas_call(unpack_kernel, out_shape=jax.ShapeDtypeStruct(queries.shap...]
    pallas_call x1, Pallas kernels: 89 us -> 90 us  [shards(): pl.pallas_call(main_kernel, out_shape=jax.ShapeDtypeStruct(BLOCK, jnp.bfl...]
where the time goes in v5:
time: 92.5 us; the launch traced here: 92.3 us
  Pallas kernels  92.3 us (100%)
    pallas_call x1, Pallas kernels, shards(): pl.pallas_call(main_kernel, out_shape=jax.ShapeDtypeStruct(BLOCK, jnp.bfl...  90 us
    pallas_call x1, Pallas kernels, shards(): pl.pallas_call(unpack_kernel, out_shape=jax.ShapeDtypeStruct(queries.shap...  2.3 us

profile of v5, /device:TPU:1, one launch (start us, length us, event | category | flops | bytes accessed | tf_op | source)
XLA Modules:
  0.0 92.3 jit_solution(10224679257541825133)
XLA Ops:
  0.0 90.0 %dispatch_attend_return.1 = bf16[8,8,16,2,128]{4,3,2,1,0:T(2,128)(2,1)} custom-call(s32[1,4]{1,0:T(1,128)} %len_ref.1, s32[16,64]{1,0:T(8,128)} %bitcast.3, bf16[64,4096]{1,0:T(8,128)(2,1)} %q_ref.1, bf16[64,4096]{1,0:T(8,128)(2,1)} %k_ref.1, bf16[64,4096]{1,0:T(8,128)(2,1)} %v_ref.1), custom_call_target="tpu_custom_call" | custom-call | tf_op jit(solution)/shard_map/dispatch_attend_return/pallas_call | solution.py:340
  90.0 2.3 %unpack.1 = bf16[64,4096]{1,0:T(8,128)(2,1)} custom-call(s32[16,64]{1,0:T(8,128)} %bitcast.4, bf16[2048,128]{1,0:T(8,128)(2,1)} %bitcast.2), custom_call_target="tpu_custom_call" | custom-call | tf_op jit(solution)/shard_map/unpack/pallas_call | solution.py:360
